TPU v7x, 32 devices: a whole 2x2x4 slice. The times are simulated.
32 devices in a mesh: groups: 2 (over x), dom: 16 (over z, y, core).
Axes of the slice: x: 2, y: 2, z: 4, core: 2. Of those that a mesh axis runs over, the one named last changes fastest.
Arguments:
- micrographs: bfloat16 [64, 1024, 1024], P(('groups', 'dom')), parts along dimension 0, may hold values from -6 to 6
- mic_defocus: int32 [64], P(('groups', 'dom')), parts along dimension 0, may hold values from 0 to 15
- defocus: float32 [32], P('groups'), parts along dimension 0, may hold values from 0.5 to 3
- pick_list: int32 [4, 6144], P(None, ('groups', 'dom')), parts along dimension 1, may hold values from -1 to 1535, as said below
- template_bank: bfloat16 [448, 2048], P(('groups', 'dom')), parts along dimension 0, may hold values from -0.125 to 0.125
- rot_index: int32 [100, 36], P('groups'), parts along dimension 0, may hold values from 0 to 223, as said below
Outputs:
- correlation: bfloat16 [3072, 16, 1800], P(('groups', 'dom')), parts along dimension 0
There are 2 independent parts, one for each index of `groups`. A program takes and returns all parts, laid end to end along the dimension named above; each array names one. Nothing has to cross between parts.
Inputs may be any that keep to these rules, and one draw needn't show every extreme that they name: `pick_list`: row 0 is a micrograph of the device that holds the column (its local index), rows 1 and 2 the top-left pixel of a 256 x 256 box inside it, row 3 the particle the box becomes or -1 for an unused column. Every particle is named by exactly one column. The used columns of one device that name particles of one device number 0 or exactly 12; a device has at most 192 used columns, reached on a quarter of the devices. `rot_index`: every bank entry is named at least once.
All inputs are finite; a program needn't handle non-finite values.
Results may differ from a plain program's by a relative error of at most 0.0071.
Values may be sent and summed in bfloat16 or wider, within the bound.
A program may use at most 128 MiB of HBM per device.

v0:
```python
import math

import jax
import jax.numpy as jnp
from jax import lax
from jax.sharding import PartitionSpec as P

BOX = 256
K = 32
SH = 4
DEFOCI = 16
P_DEV = 96
SHIFTS = 16
PICK_CAP = 192


TWO_PI = 2.0 * math.pi
CHI_SCALE = 0.05
CHI_SHIFT = 0.1


def forward_table(box_side, freq_side):
    offsets = jnp.arange(freq_side, dtype=jnp.int32) - freq_side // 2
    pixels = jnp.arange(box_side, dtype=jnp.int32)
    phase_turns = (
        jnp.mod(offsets[:, None] * pixels[None, :], box_side).astype(jnp.float32) / box_side
    )
    norm_scale = 1.0 / math.sqrt(box_side)
    stacked = jnp.concatenate(
        [jnp.cos(TWO_PI * phase_turns) * norm_scale, -jnp.sin(TWO_PI * phase_turns) * norm_scale],
        axis=0,
    )
    return stacked.astype(jnp.bfloat16)


def ctf_table(defocus, freq_side):
    offsets = (jnp.arange(freq_side, dtype=jnp.int32) - freq_side // 2).astype(jnp.float32)
    radius = (offsets[:, None] * offsets[:, None] + offsets[None, :] * offsets[None, :]).reshape(-1)
    return -jnp.sin(CHI_SCALE * defocus[:, None] * radius[None, :] + CHI_SHIFT)


def shift_tables(box_side, freq_side, shift_side):
    offsets = jnp.arange(freq_side, dtype=jnp.int32) - freq_side // 2
    shift_moves = jnp.arange(shift_side, dtype=jnp.int32) - shift_side // 2
    row_freq = jnp.repeat(offsets, freq_side)
    col_freq = jnp.tile(offsets, freq_side)
    row_move = jnp.repeat(shift_moves, shift_side)
    col_move = jnp.tile(shift_moves, shift_side)
    phase_turns = (
        jnp.mod(
            row_move[:, None] * row_freq[None, :] + col_move[:, None] * col_freq[None, :], box_side
        ).astype(jnp.float32)
        / box_side
    )
    return (jnp.cos(TWO_PI * phase_turns), jnp.sin(TWO_PI * phase_turns))


def shift_rows(window, cosine, sine_part, freq_side):
    box_count = window.shape[0]
    freq_area = freq_side * freq_side
    real_w = window[:, :freq_area].astype(jnp.float32)[:, None, :]
    imag_w = window[:, freq_area:].astype(jnp.float32)[:, None, :]
    real_s = real_w * cosine[None] - imag_w * sine_part[None]
    imag_s = real_w * sine_part[None] + imag_w * cosine[None]
    joined = jnp.concatenate([real_s, imag_s], axis=2).astype(jnp.bfloat16)
    return joined.reshape(box_count * cosine.shape[0], 2 * freq_area)


def body(micrographs, mic_defocus, defocus, pick_list, template_bank, rot_index):
    peer_count = lax.axis_size("dom")
    slot_cap = (P_DEV + peer_count - 1) // peer_count * 2
    mic_count = micrographs.shape[0]
    freq_area = K * K
    dft_table = forward_table(BOX, K)
    ctf_all = ctf_table(defocus, K)
    cosine, sine_part = shift_tables(BOX, K, SH)
    per_block = min(32, PICK_CAP)

    def crop_one(mic_id, top_row, left_col):
        return lax.dynamic_slice(micrographs, (mic_id, top_row, left_col), (1, BOX, BOX))[0]

    def window_block(block_args):
        mic_b, top_b, left_b = block_args
        box_stack = jax.vmap(crop_one)(mic_b, top_b, left_b)
        mic_match = mic_b[:, None] == jnp.arange(mic_count, dtype=jnp.int32)[None, :]
        defocus_ids = jnp.sum(jnp.where(mic_match, mic_defocus[None, :], 0), axis=1)
        class_match = (
            defocus_ids[:, None, None] == jnp.arange(DEFOCI, dtype=jnp.int32)[None, :, None]
        )
        ctf_rows = jnp.sum(jnp.where(class_match, ctf_all[None], 0.0), axis=1)
        first_pass = jnp.einsum(
            "ky,byx->bkx", dft_table, box_stack, preferred_element_type=jnp.float32
        ).astype(jnp.bfloat16)
        second = jnp.einsum(
            "bkx,jx->bkj", first_pass, dft_table, preferred_element_type=jnp.float32
        )
        real_part = second[:, :K, :K] - second[:, K:, K:]
        imag_part = second[:, :K, K:] + second[:, K:, :K]
        box_count = box_stack.shape[0]
        joined = jnp.concatenate(
            [
                real_part.reshape(box_count, -1) * ctf_rows,
                imag_part.reshape(box_count, -1) * ctf_rows,
            ],
            axis=1,
        )
        return joined.astype(jnp.bfloat16)

    windows = lax.map(
        window_block,
        (
            pick_list[0].reshape(-1, per_block),
            pick_list[1].reshape(-1, per_block),
            pick_list[2].reshape(-1, per_block),
        ),
    )
    windows = windows.reshape(PICK_CAP, 2 * freq_area)
    target_index = pick_list[3]
    is_live = target_index >= 0
    target_dev = jnp.where(is_live, target_index // P_DEV, -1)
    target_slot = jnp.mod(target_index, P_DEV)
    columns = jnp.arange(PICK_CAP, dtype=jnp.int32)
    earlier = (
        (columns[None, :] < columns[:, None])
        & (target_dev[None, :] == target_dev[:, None])
        & is_live[None, :]
    )
    order_rank = jnp.sum(earlier.astype(jnp.int32), axis=1)
    position = jnp.where(is_live, target_dev * slot_cap + order_rank, -1)
    slot_ids = jnp.arange(peer_count * slot_cap, dtype=jnp.int32)
    slot_match = position[None, :] == slot_ids[:, None]
    outgoing = jnp.dot(
        slot_match.astype(jnp.bfloat16), windows, preferred_element_type=jnp.float32
    ).astype(jnp.bfloat16)
    slot_labels = jnp.sum(jnp.where(slot_match, target_slot[None, :] + 1, 0), axis=1).astype(
        jnp.bfloat16
    )
    arrived, arrived_labels = (
        lax.all_to_all(outgoing, "dom", split_axis=0, concat_axis=0, tiled=True),
        lax.all_to_all(slot_labels, "dom", split_axis=0, concat_axis=0, tiled=True),
    )
    placing = (
        arrived_labels.astype(jnp.float32)[None, :]
        == (jnp.arange(P_DEV, dtype=jnp.int32) + 1).astype(jnp.float32)[:, None]
    )
    particle_windows = jnp.dot(
        placing.astype(jnp.bfloat16), arrived, preferred_element_type=jnp.float32
    ).astype(jnp.bfloat16)
    shifted = shift_rows(particle_windows, cosine, sine_part, K)
    flat_index = rot_index.reshape(-1)
    contract = (((1,), (1,)), ((), ()))
    bank_piece = lax.all_gather(template_bank, "dom", axis=0, tiled=True)
    part_scores = lax.dot_general(shifted, bank_piece, contract, preferred_element_type=jnp.float32)
    all_scores = part_scores.astype(jnp.bfloat16).reshape(P_DEV, SHIFTS, bank_piece.shape[0])
    correlation = jnp.take(all_scores, flat_index, axis=2)
    return correlation


def solution(mesh):
    return jax.shard_map(
        body,
        mesh=mesh,
        in_specs=(
            P(("groups", "dom"), None, None),
            P(("groups", "dom")),
            P("groups"),
            P(None, ("groups", "dom")),
            P(("groups", "dom"), None),
            P("groups", None),
        ),
        out_specs=P(("groups", "dom"), None, None),
        check_vma=False,
    )
```

profile of v0, /device:TPU:27, one launch (start us, length us, event | category | flops | bytes accessed | tf_op | source)
XLA Modules:
  0.0 940.4 jit_solution(5439050297436248444)
XLA Ops:
  3.3 6.4 all-to-all-start
  11.0 849.9 %while.15 = (s32[]{:T(128)}, bf16[6,32,2048]{2,1,0:T(8,128)(2,1)S(1)}, s32[6,32]{1,0:T(8,128)S(1)}, s32[6,32]{1,0:T(8,128)S(1)}, s32[6,32]{1,0:T(8,128)S(1)}, /*...) while((s32[]{:T(128)}, ...), condition=%wide.region_5.6_spmd.clone, body=%wide.region_2.5_spmd.clone.sunk | while | flops 337593472 | bytes 7382026 | solution.py:109
  12.6 135.8 %while.16 = (s32[]{:T(128)}, bf16[2,1024,1024]{2,1,0:T(8,128)(2,1)}, s32[32,3]{0,1:T(4,128)S(1)}, bf16[32,1,256,256]{3,2,1,0:T(8,128)(2,1)}, s32[]{:T(128)}) while((s32[]{:T(128)}, bf16[2,1024,1024]{2,1,0:T(8,128)(2,1)}, s32[32,3]{0,1:T(4,128)S(1)}, bf16[32,1,256,256]{3,2,1,0:T(8,128)(2,1)}, s32[]{:T(128)}) %tuple.60), condition=%wide.while_cond, body=%wide.while_body.sunk | while | flops 2 | bytes 263805 | solution.py:80
  13.3 3.6 bitcast_dynamic-update-slice_fusion.2
  21.8 3.6 bitcast_dynamic-update-slice_fusion.2
  30.2 3.6 bitcast_dynamic-update-slice_fusion.2
  34.5 3.6 bitcast_dynamic-update-slice_fusion.2
  38.7 3.6 bitcast_dynamic-update-slice_fusion.2
  43.0 3.6 bitcast_dynamic-update-slice_fusion.2
  51.5 3.6 bitcast_dynamic-update-slice_fusion.2
  59.9 3.6 bitcast_dynamic-update-slice_fusion.2
  64.2 3.6 bitcast_dynamic-update-slice_fusion.2
  68.4 3.6 bitcast_dynamic-update-slice_fusion.2
  72.7 3.6 bitcast_dynamic-update-slice_fusion.2
  81.1 3.6 bitcast_dynamic-update-slice_fusion.2
  89.6 3.6 bitcast_dynamic-update-slice_fusion.2
  93.9 3.6 bitcast_dynamic-update-slice_fusion.2
  102.4 3.6 bitcast_dynamic-update-slice_fusion.2
  110.8 3.6 bitcast_dynamic-update-slice_fusion.2
  115.1 3.6 bitcast_dynamic-update-slice_fusion.2
  119.3 3.6 bitcast_dynamic-update-slice_fusion.2
  123.6 3.6 bitcast_dynamic-update-slice_fusion.2
  132.1 3.6 bitcast_dynamic-update-slice_fusion.2
  140.5 3.6 bitcast_dynamic-update-slice_fusion.2
  144.8 3.6 bitcast_dynamic-update-slice_fusion.2
  154.2 135.8 %while.16 = (s32[]{:T(128)}, bf16[2,1024,1024]{2,1,0:T(8,128)(2,1)}, s32[32,3]{0,1:T(4,128)S(1)}, bf16[32,1,256,256]{3,2,1,0:T(8,128)(2,1)}, s32[]{:T(128)}) while((s32[]{:T(128)}, bf16[2,1024,1024]{2,1,0:T(8,128)(2,1)}, s32[32,3]{0,1:T(4,128)S(1)}, bf16[32,1,256,256]{3,2,1,0:T(8,128)(2,1)}, s32[]{:T(128)}) %tuple.60), condition=%wide.while_cond, body=%wide.while_body.sunk | while | flops 2 | bytes 263805 | solution.py:80
  154.9 3.6 bitcast_dynamic-update-slice_fusion.2
  159.2 3.6 bitcast_dynamic-update-slice_fusion.2
  163.4 3.6 bitcast_dynamic-update-slice_fusion.2
  167.6 3.6 bitcast_dynamic-update-slice_fusion.2
  176.1 3.6 bitcast_dynamic-update-slice_fusion.2
  184.6 3.6 bitcast_dynamic-update-slice_fusion.2
  188.9 3.6 bitcast_dynamic-update-slice_fusion.2
  193.1 3.6 bitcast_dynamic-update-slice_fusion.2
  197.3 3.6 bitcast_dynamic-update-slice_fusion.2
  205.8 3.6 bitcast_dynamic-update-slice_fusion.2
  214.3 3.6 bitcast_dynamic-update-slice_fusion.2
  218.6 3.6 bitcast_dynamic-update-slice_fusion.2
  227.0 3.6 bitcast_dynamic-update-slice_fusion.2
  295.9 135.8 %while.16 = (s32[]{:T(128)}, bf16[2,1024,1024]{2,1,0:T(8,128)(2,1)}, s32[32,3]{0,1:T(4,128)S(1)}, bf16[32,1,256,256]{3,2,1,0:T(8,128)(2,1)}, s32[]{:T(128)}) while((s32[]{:T(128)}, bf16[2,1024,1024]{2,1,0:T(8,128)(2,1)}, s32[32,3]{0,1:T(4,128)S(1)}, bf16[32,1,256,256]{3,2,1,0:T(8,128)(2,1)}, s32[]{:T(128)}) %tuple.60), condition=%wide.while_cond, body=%wide.while_body.sunk | while | flops 2 | bytes 263805 | solution.py:80
  437.6 135.8 %while.16 = (s32[]{:T(128)}, bf16[2,1024,1024]{2,1,0:T(8,128)(2,1)}, s32[32,3]{0,1:T(4,128)S(1)}, bf16[32,1,256,256]{3,2,1,0:T(8,128)(2,1)}, s32[]{:T(128)}) while((s32[]{:T(128)}, bf16[2,1024,1024]{2,1,0:T(8,128)(2,1)}, s32[32,3]{0,1:T(4,128)S(1)}, bf16[32,1,256,256]{3,2,1,0:T(8,128)(2,1)}, s32[]{:T(128)}) %tuple.60), condition=%wide.while_cond, body=%wide.while_body.sunk | while | flops 2 | bytes 263805 | solution.py:80
  579.2 135.8 %while.16 = (s32[]{:T(128)}, bf16[2,1024,1024]{2,1,0:T(8,128)(2,1)}, s32[32,3]{0,1:T(4,128)S(1)}, bf16[32,1,256,256]{3,2,1,0:T(8,128)(2,1)}, s32[]{:T(128)}) while((s32[]{:T(128)}, bf16[2,1024,1024]{2,1,0:T(8,128)(2,1)}, s32[32,3]{0,1:T(4,128)S(1)}, bf16[32,1,256,256]{3,2,1,0:T(8,128)(2,1)}, s32[]{:T(128)}) %tuple.60), condition=%wide.while_cond, body=%wide.while_body.sunk | while | flops 2 | bytes 263805 | solution.py:80
  720.9 135.8 %while.16 = (s32[]{:T(128)}, bf16[2,1024,1024]{2,1,0:T(8,128)(2,1)}, s32[32,3]{0,1:T(4,128)S(1)}, bf16[32,1,256,256]{3,2,1,0:T(8,128)(2,1)}, s32[]{:T(128)}) while((s32[]{:T(128)}, bf16[2,1024,1024]{2,1,0:T(8,128)(2,1)}, s32[32,3]{0,1:T(4,128)S(1)}, bf16[32,1,256,256]{3,2,1,0:T(8,128)(2,1)}, s32[]{:T(128)}) %tuple.60), condition=%wide.while_cond, body=%wide.while_body.sunk | while | flops 2 | bytes 263805 | solution.py:80
  862.4 6.0 all-to-all-start.1
  869.2 37.2 %all-gather = bf16[16,14,2048]{2,1,0:T(8,128)(2,1)S(1)} all-gather(bf16[1,14,2048]{2,1,0:T(8,128)(2,1)S(1)} %bitcast.81), channel_id=1, replica_groups=mesh['groups'=2,'dom'=16] {'dom'}, dimensions={0}, use_global_device_ids=true | all-gather | bytes 974848 | tf_op jit(solution)/shard_map/all_gather | solution.py:152
  913.7 6.9 gather_fusion
  920.5 8.6 select_bitcast_fusion
  929.1 11.2 %copy.23 = bf16[96,16,1800]{2,1,0:T(8,128)(2,1)} copy(bf16[96,16,1800]{0,1,2:T(8,128)(2,1)} %select_bitcast_fusion) | data formatting | bytes 11059200 | tf_op jit(solution)/shard_map/jit(_take)/select_n | solution.py:155
  (685 shorter events, 737.3 us)
Async XLA Ops:
  3.3 859.1 %all-to-all-start = ((bf16[16,12,1]{1,2,0:T(2,128)(2,1)}), bf16[16,12,1]{1,2,0:T(2,128)(2,1)S(1)}, u32[]{:S(2)}, u32[]{:S(2)}) async-start(bf16[16,12,1]{1,2,0:T(2,128)(2,1)} %convert_element_type.116), calls=%async_computation | async-start | bytes 16384 | tf_op jit(solution)/shard_map/all_to_all | solution.py:140
  860.8 7.6 copy-start.1
  860.9 8.4 copy-start
  862.4 44.9 %all-to-all-start.1 = ((bf16[16,12,2048]{2,1,0:T(8,128)(2,1)}), bf16[16,12,2048]{2,1,0:T(8,128)(2,1)S(1)}, u32[]{:S(2)}, u32[]{:S(2)}) async-start(bf16[16,12,2048]{2,1,0:T(8,128)(2,1)} %all_to_all.13), calls=%async_computation.1 | async-start | bytes 2097152 | tf_op jit(solution)/shard_map/all_to_all | solution.py:139
where the time goes:
time: 954 us; the launch traced here: 940 us
  local copies, waits for them, and re-layouts  840 us (88%)
  blocking collectives  37.2 us (4%)
  other arithmetic  26.5 us (3%)
  matrix products  23 us (2%)
  starting transfers between devices  12.4 us (1%)
    gather x576, local copies, waits for them, and re-layouts  814 us
    all_gather x1, blocking collectives, body(): bank_piece = lax.all_gather(template_bank, 'dom', axis=0, tiled=True)  37.2 us
    dot_general x6, matrix products, window_block(): jnp.einsum('bkx,jx->bkj', first_pass, dft_table, preferred_element_type=j...  19.9 us
  transfers between devices with their start and end apart: 2, of which 0 were waited for; matrix products, arithmetic and copies ran while one was open for 91% of the time, Pallas kernels for 0%

commit v1 on v0

v1 whole, which is shorter than its diff:
```python
import functools
import math

import jax
import jax.numpy as jnp
import ml_dtypes
import numpy as np
from jax import lax
from jax.experimental import pallas as pl
from jax.experimental.pallas import tpu as pltpu
from jax.sharding import PartitionSpec as P

BOX = 256
K = 32
SH = 4
P_DEV = 96
SHIFTS = SH * SH
LANES = 128
ROWS = 16
GROUP = 4
CHUNK = 16

TWO_PI = 2.0 * math.pi
CHI_SCALE = 0.05
CHI_SHIFT = 0.1

SUB = np.arange(8)[:, None]
LANE = np.arange(LANES)[None, :]
TILE_U = (8 * (LANE // K) + SUB - K // 2).astype(np.float64)
TILE_V = (LANE % K + 0 * SUB - K // 2).astype(np.float64)


def dft_tables():
    freq = np.arange(K) - K // 2
    phase = TWO_PI * np.mod(freq[:, None] * np.arange(BOX)[None, :], BOX) / BOX
    cosine = np.cos(phase) / math.sqrt(BOX)
    sine = -np.sin(phase) / math.sqrt(BOX)
    left = np.concatenate([cosine, sine], axis=0)
    right = np.zeros((GROUP, BOX, 2 * GROUP * K))
    for j in range(GROUP):
        right[j, :, j * K : (j + 1) * K] = cosine.T
        right[j, :, GROUP * K + j * K : GROUP * K + (j + 1) * K] = sine.T
    right = right.reshape(GROUP * BOX, 2 * GROUP * K)
    return left.astype(np.float32).astype(ml_dtypes.bfloat16), right.astype(np.float32).astype(ml_dtypes.bfloat16)


def phase_tables():
    rows = TWO_PI * np.arange(ROWS)[:, None, None] * TILE_U[None] / BOX
    cols = TWO_PI * np.arange(LANES)[:, None] * TILE_V[:1] / BOX
    return [f(x).astype(np.float32) for x in (rows, cols) for f in (np.cos, np.sin)]


def shift_phases():
    moves = np.arange(SH) - SH // 2
    row_move = np.repeat(moves, SH)[None, :, None]
    col_move = np.tile(moves, SH)[None, :, None]
    phase = TWO_PI * (TILE_U[:, None, :] * row_move + TILE_V[:, None, :] * col_move) / BOX
    return np.cos(phase).astype(np.float32), np.sin(phase).astype(np.float32)


def bits(n):
    return (n - 1).bit_length()


def window_tiles(q, base, slot_cap, label_bits, row_bits, col_bits, info, mic_def, mic, lane_id, row_id, lhs):
    scalars = []
    last_tile = mic.shape[1] // ROWS - 1
    last_block = mic.shape[2] // LANES - 1
    for j in range(GROUP):
        packed = lax.shift_right_logical(info[base + j], label_bits)
        left = packed & (2**col_bits - 1)
        top = lax.shift_right_logical(packed, col_bits) & (2**row_bits - 1)
        m = lax.shift_right_logical(packed, col_bits + row_bits)
        block, rl = lax.shift_right_logical(left, 7), left & (LANES - 1)
        tile, rt = lax.shift_right_logical(top, 4), top & (ROWS - 1)
        end_tile = jnp.minimum(tile + BOX // ROWS, last_tile)
        row_f = rt.astype(jnp.float32).astype(jnp.bfloat16)
        col_f = rl.astype(jnp.float32).astype(jnp.bfloat16)

        def column(b):
            lanes = pl.ds(pl.multiple_of(b * LANES, LANES), LANES)
            main = mic[m, pl.ds(pl.multiple_of(tile * ROWS, ROWS), BOX), lanes]
            tail = mic[m, pl.ds(pl.multiple_of(end_tile * ROWS, ROWS), ROWS), lanes]
            head = jnp.where(row_id[...] >= row_f, main[:ROWS], tail)
            return jnp.concatenate([head, main[ROWS:]], axis=0)

        first = column(block)
        third = column(jnp.minimum(block + 2, last_block))
        mask = jnp.broadcast_to(lane_id[...], (BOX, LANES)) >= col_f
        lhs[pl.ds(q * BOX, BOX), pl.ds(2 * j * LANES, LANES)] = jnp.where(mask, first, third)
        lhs[pl.ds(q * BOX, BOX), pl.ds((2 * j + 1) * LANES, LANES)] = column(block + 1)
        scalars.append((m, rt, rl))
    return scalars


def group_windows(grid_part, scalars, left_t, prow_c, prow_s, pcol_c, pcol_s, ctf, mic_def):
    second = jnp.dot(left_t[...], grid_part.astype(jnp.bfloat16), preferred_element_type=jnp.float32)
    real = second[:K, :LANES] - second[K:, LANES:]
    imag = second[:K, LANES:] + second[K:, :LANES]
    block_id = lax.broadcasted_iota(jnp.int32, (8, LANES), 1) // K
    tiles = []
    for j in range(GROUP):
        parts = []
        for x in (real, imag):
            total = None
            for k in range(K // 8):
                piece = x[8 * k : 8 * k + 8]
                shift = (K * (k - j)) % LANES
                piece = pltpu.roll(piece, shift, 1) if shift else piece
                total = piece if total is None else jnp.where(block_id == k, piece, total)
            parts.append(total)
        m, rt, rl = scalars[j]
        cu, su = prow_c[rt], prow_s[rt]
        cv = jnp.broadcast_to(pcol_c[pl.ds(rl, 1), :], (8, LANES))
        sv = jnp.broadcast_to(pcol_s[pl.ds(rl, 1), :], (8, LANES))
        weight = ctf[mic_def[m]]
        a = (cu * cv - su * sv) * weight
        b = (su * cv + cu * sv) * weight
        tiles.append(
            jnp.concatenate(
                [parts[0] * a - parts[1] * b, parts[0] * b + parts[1] * a], axis=0
            ).astype(jnp.bfloat16)
        )
    return tiles


def crop_kernel(peers, slot_cap, shifts, info, mic_def, labels, mic, left_t, right_t, prow_c, prow_s,
                pcol_c, pcol_s, ctf, lane_id, row_id, out, lhs):
    groups = slot_cap // GROUP

    def per_peer(peer, carry):
        scalars = [
            window_tiles(q, peer * slot_cap + q * GROUP, slot_cap, *shifts, info, mic_def, mic,
                         lane_id, row_id, lhs)
            for q in range(groups)
        ]
        first = jnp.dot(lhs[...], right_t[...], preferred_element_type=jnp.float32)
        for q in range(groups):
            tiles = group_windows(first[q * BOX : (q + 1) * BOX], scalars[q], left_t, prow_c, prow_s,
                                  pcol_c, pcol_s, ctf, mic_def)
            for j in range(GROUP):
                out[peer, q * GROUP + j] = tiles[j]
        out[peer, slot_cap] = labels[peer]
        return carry

    lax.fori_loop(0, peers, per_peer, 0)


def score_kernel(where, arrived, bank, pick, cos_t, sin_t, out, lhs):
    base = pl.program_id(0) * CHUNK

    def expand(n, carry):
        x = arrived[where[base + n]].astype(jnp.float32)
        rows = pl.ds(pl.multiple_of(n * SHIFTS, SHIFTS), SHIFTS)
        for k in range(8):
            re = jnp.broadcast_to(x[k : k + 1], (SHIFTS, LANES))
            im = jnp.broadcast_to(x[8 + k : 9 + k], (SHIFTS, LANES))
            c, s = cos_t[k], sin_t[k]
            lhs[rows, k * LANES : (k + 1) * LANES] = (re * c - im * s).astype(jnp.bfloat16)
            lhs[rows, (8 + k) * LANES : (9 + k) * LANES] = (re * s + im * c).astype(jnp.bfloat16)
        return carry

    lax.fori_loop(0, CHUNK, expand, 0, unroll=2)
    scores = lax.dot_general(lhs[...], bank[...], (((1,), (1,)), ((), ())),
                             preferred_element_type=jnp.float32).astype(jnp.bfloat16)
    out[...] = jnp.dot(scores, pick[...], preferred_element_type=jnp.float32).astype(jnp.bfloat16)


VMEM = pl.BlockSpec(memory_space=pltpu.VMEM)
SMEM = pl.BlockSpec(memory_space=pltpu.SMEM)


def body(micrographs, mic_defocus, defocus, pick_list, template_bank, rot_index):
    peers = lax.axis_size("dom")
    slot_cap = (P_DEV + peers - 1) // peers * 2
    slot_cap = -(-slot_cap // GROUP) * GROUP
    mics, height, width = micrographs.shape
    label_bits, row_bits, col_bits = bits(P_DEV + 1), bits(height), bits(width)
    columns = pick_list.shape[1]

    target = pick_list[3]
    live = target >= 0
    target_dev = jnp.where(live, target // P_DEV, -1)
    label = jnp.where(live, jnp.mod(target, P_DEV) + 1, 0)
    ids = jnp.arange(columns, dtype=jnp.int32)
    earlier = (ids[None, :] < ids[:, None]) & (target_dev[None, :] == target_dev[:, None])
    rank = jnp.sum(earlier.astype(jnp.int32), axis=1)
    position = jnp.where(live, target_dev * slot_cap + rank, -1)
    mic_id = jnp.clip(pick_list[0], 0, mics - 1)
    top = jnp.clip(pick_list[1], 0, height - BOX)
    left = jnp.clip(pick_list[2], 0, width - BOX)
    packed = (((mic_id << row_bits) + top << col_bits) + left << label_bits) + label
    slots = jnp.arange(peers * slot_cap, dtype=jnp.int32)
    info = jnp.sum(jnp.where(position[None, :] == slots[:, None], packed[None, :], 0), axis=1)
    labels = (info & (2**label_bits - 1)).astype(jnp.bfloat16).reshape(peers, 1, slot_cap)
    labels = jnp.broadcast_to(jnp.pad(labels, ((0, 0), (0, 0), (0, LANES - slot_cap))), (peers, ROWS, LANES))

    left_t, right_t = dft_tables()
    radius = jnp.asarray((TILE_U**2 + TILE_V**2).astype(np.float32))
    ctf = -jnp.sin(CHI_SCALE * defocus[:, None, None] * radius[None] + CHI_SHIFT)
    lane_id = np.broadcast_to(np.arange(LANES, dtype=np.float32), (ROWS, LANES)).astype(ml_dtypes.bfloat16)
    row_id = np.broadcast_to(np.arange(ROWS, dtype=np.float32)[:, None], (ROWS, LANES)).astype(ml_dtypes.bfloat16)

    groups = slot_cap // GROUP
    outgoing = pl.pallas_call(
        functools.partial(crop_kernel, peers, slot_cap, (label_bits, row_bits, col_bits)),
        out_shape=jax.ShapeDtypeStruct((peers, slot_cap + 1, ROWS, LANES), jnp.bfloat16),
        in_specs=[SMEM, SMEM] + [VMEM] * 11,
        out_specs=VMEM,
        scratch_shapes=[pltpu.VMEM((groups * BOX, GROUP * BOX), jnp.bfloat16)],
        compiler_params=pltpu.CompilerParams(vmem_limit_bytes=48 << 20),
        name="crop",
    )(info, mic_defocus, labels, micrographs, jnp.asarray(left_t), jnp.asarray(right_t),
      *[jnp.asarray(t) for t in phase_tables()], ctf, jnp.asarray(lane_id[:1]), jnp.asarray(row_id))

    bank_rows, area2 = template_bank.shape
    pad_rows = -(-bank_rows // ROWS) * ROWS
    shard = template_bank.reshape(bank_rows, 2, K // 8, 8, K).transpose(0, 1, 3, 2, 4).reshape(bank_rows, area2)
    shard = jnp.pad(shard, ((0, pad_rows - bank_rows), (0, 0)))

    arrived = lax.all_to_all(outgoing, "dom", split_axis=0, concat_axis=0, tiled=True)
    bank = lax.all_gather(shard, "dom", axis=0, tiled=True)

    stride = slot_cap + 1
    got = arrived[:, slot_cap, 0, :slot_cap].astype(jnp.int32)
    at = jnp.arange(peers, dtype=jnp.int32)[:, None] * stride + jnp.arange(slot_cap, dtype=jnp.int32)[None, :]
    wanted = jnp.arange(P_DEV, dtype=jnp.int32) + 1
    where = jnp.sum(jnp.where(got[None] == wanted[:, None, None], at[None], 0), axis=(1, 2))

    flat = rot_index.reshape(-1)
    entry = flat // bank_rows * pad_rows + flat % bank_rows
    templates = flat.shape[0]
    pick = (jnp.arange(peers * pad_rows, dtype=jnp.int32)[:, None] == entry[None, :]).astype(jnp.bfloat16)

    cos_t, sin_t = shift_phases()
    full = lambda shape: pl.BlockSpec(shape, lambda i: (0,) * len(shape), pipeline_mode=pl.Buffered(1))
    out = pl.pallas_call(
        score_kernel,
        grid=(P_DEV // CHUNK,),
        out_shape=jax.ShapeDtypeStruct((P_DEV * SHIFTS, templates), jnp.bfloat16),
        in_specs=[
            SMEM,
            full((peers * stride, ROWS, LANES)),
            full((peers * pad_rows, area2)),
            full((peers * pad_rows, templates)),
            full((8, SHIFTS, LANES)),
            full((8, SHIFTS, LANES)),
        ],
        out_specs=pl.BlockSpec((CHUNK * SHIFTS, templates), lambda i: (i, 0)),
        scratch_shapes=[pltpu.VMEM((CHUNK * SHIFTS, area2), jnp.bfloat16)],
        compiler_params=pltpu.CompilerParams(vmem_limit_bytes=48 << 20),
        name="score",
    )(where, arrived.reshape(peers * stride, ROWS, LANES), bank, pick, jnp.asarray(cos_t), jnp.asarray(sin_t))
    return out.reshape(P_DEV, SHIFTS, templates)


def solution(mesh):
    return jax.shard_map(
        body,
        mesh=mesh,
        in_specs=(
            P(("groups", "dom"), None, None),
            P(("groups", "dom")),
            P("groups"),
            P(None, ("groups", "dom")),
            P(("groups", "dom"), None),
            P("groups", None),
        ),
        out_specs=P(("groups", "dom"), None, None),
        check_vma=False,
    )
```

time: 954 us -> 92 us (0.10)
  the two profiles are of different devices: /device:TPU:27 before, /device:TPU:9 now
where the time goes in v1:
time: 92 us; the launch traced here: 91.2 us
  Pallas kernels  32.9 us (36%)
  waiting for transfers between devices  20.1 us (22%)
  between operations  13.6 us (15%)
  local copies, waits for them, and re-layouts  13.4 us (15%)
  starting transfers between devices  6.64 us (7%)
  other arithmetic  4.61 us (5%)
    pallas_call x1, Pallas kernels, body(): pl.pallas_call(functools.partial(crop_kernel, peers, slot_cap, (label_bit...  20.9 us
    all_to_all x1, waiting for transfers between devices, body(): lax.all_to_all(outgoing, 'dom', split_axis=0, concat_axis=0, tiled=True)  20 us
    pallas_call x1, Pallas kernels, body(): pl.pallas_call(score_kernel, grid=(P_DEV // CHUNK,), out_shape=jax.ShapeD...  12 us
    unnamed x28, local copies, waits for them, and re-layouts  10.6 us
    all_to_all x1, starting transfers between devices, body(): lax.all_to_all(outgoing, 'dom', split_axis=0, concat_axis=0, tiled=True)  6.64 us
  transfers between devices with their start and end apart: 2, of which 1 were waited for; matrix products, arithmetic and copies ran while one was open for 6% of the time, Pallas kernels for 23%

profile of v1, /device:TPU:9, one launch (start us, length us, event | category | flops | bytes accessed | tf_op | source)
XLA Modules:
  0.0 91.2 jit_solution(16920593769757816461)
XLA Ops:
  6.5 0.0 all-gather.2.cloned.1.call-start
  6.5 1.0 %reshape.136 = bf16[14,2,4,8,32]{4,3,2,1,0:T(8,128)(2,1)S(1)} reshape(bf16[14,2048]{1,0:T(8,128)(2,1)} %param.21) | data formatting | bytes 114688 | tf_op jit(solution)/shard_map/reshape | solution.py:218
  7.6 0.1 copy.29
  7.7 0.0 copy-start.13
  7.7 0.2 reshape.137
  8.0 0.6 pad.9
  8.6 0.0 all-gather.2.cloned.1.call-update
  8.6 0.7 fusion.10
  9.3 0.7 fusion.4
  10.0 0.7 broadcast_multiply_fusion
  10.7 0.2 convert_reduce_fusion
  10.9 0.9 add_select_fusion.4
  11.7 0.1 select_reduce_fusion.info
  11.9 0.1 convert_element_type.35
  12.0 1.0 %sine_negate_fusion.ctf = f32[16,8,128]{2,1,0:T(8,128)S(1)} fusion(f32[8,128]{1,0:T(8,128)} %constant.85.clone, f32[16]{0:T(128)S(1)} %broadcast_multiply_fusion), kind=kLoop, calls=%fused_computation.9 | loop fusion | flops 49152 | bytes 69696 | tf_op jit(solution)/shard_map/neg | solution.py:200
  13.0 0.0 copy-start
  13.0 2.2 %copy-done = bf16[2,1024,1024]{2,1,0:T(8,128)(2,1)S(1)} copy-done((bf16[2,1024,1024]{2,1,0:T(8,128)(2,1)S(1)}, bf16[2,1024,1024]{2,1,0:T(8,128)(2,1)}, u32[]{:S(2)}) %copy-start) | copy-done | bytes 4194328
  15.2 0.0 copy-start.2
  15.2 1.0 %copy-done.2 = bf16[1024,256]{1,0:T(8,128)(2,1)S(1)} copy-done((bf16[1024,256]{1,0:T(8,128)(2,1)S(1)}, bf16[1024,256]{1,0:T(8,128)(2,1)}, u32[]{:S(2)}) %copy-start.2) | copy-done | bytes 524312
  16.2 0.0 copy-start.5
  16.2 0.8 copy-done.5
  17.1 0.0 copy-start.6
  17.1 0.8 copy-done.6
  17.9 0.8 copy-done.7
  18.8 0.8 copy-done.8
  19.6 0.8 copy-done.9
  20.4 0.7 copy-done.10
  21.0 0.7 copy-done.11
  21.7 0.7 copy-done.12
  22.4 20.9 %crop.1 = bf16[16,13,16,128]{3,2,1,0:T(8,128)(2,1)} custom-call(s32[192]{0:T(256)S(1)} %select_reduce_fusion.info, s32[2]{0:T(128)S(1)} %copy-done.11, bf16[16,16,128]{2,1,0:T(8,128)(2,1)S(1)} %broadcast_in_dim.57.labels, bf16[2,1024,1024]{2,1,0:T(8,128)(2,1)S(1)} %copy-done, bf16[64,256]{1,0:T(8,128)(2,1)S(1)} %copy-done.9, ...), custom_call_target="tpu_custom_call" | custom-call | tf_op jit(solution)/shard_map/crop/pallas_call | solution.py:205
  43.3 6.6 %all-to-all-start = ((bf16[16,13,16,128]{3,2,1,0:T(8,128)(2,1)}), bf16[16,13,16,128]{3,2,1,0:T(8,128)(2,1)S(1)}, u32[]{:S(2)}, u32[]{:S(2)}) async-start(bf16[16,13,16,128]{3,2,1,0:T(8,128)(2,1)} %crop.1), calls=%async_computation | async-start | bytes 1703936 | tf_op jit(solution)/shard_map/all_to_all | solution.py:221
  49.9 0.0 copy-done.13
  49.9 0.1 copy.25
  50.1 0.1 ne.79
  50.2 0.1 copy.26
  50.3 0.1 rem.46
  50.4 0.1 copy.27
  50.5 0.1 div.31
  50.6 0.2 fusion.pick
  50.8 20.0 %all-to-all-done = bf16[16,13,16,128]{3,2,1,0:T(8,128)(2,1)S(1)} async-done(((bf16[16,13,16,128]{3,2,1,0:T(8,128)(2,1)}), bf16[16,13,16,128]{3,2,1,0:T(8,128)(2,1)S(1)}, u32[]{:S(2)}, u32[]{:S(2)}) %all-to-all-start) | async-done | bytes 852000 | tf_op jit(solution)/shard_map/all_to_all | solution.py:221
  70.9 0.1 copy.23
  71.0 0.1 select_reduce_fusion.1.where
  71.1 0.0 all-gather.2.cloned.1.call-done.bank
  71.1 0.0 copy-done.3
  71.1 0.0 copy-done.4
  71.2 0.0 copy-start.1
  71.2 1.2 %copy-done.1 = bf16[256,2048]{1,0:T(8,128)(2,1)S(1)} copy-done((bf16[256,2048]{1,0:T(8,128)(2,1)S(1)}, bf16[256,2048]{1,0:T(8,128)(2,1)}, u32[]{:S(2)}) %copy-start.1) | copy-done | bytes 1048600
  72.4 12.0 %score.1 = bf16[1536,1800]{1,0:T(8,128)(2,1)} custom-call(s32[96]{0:T(128)S(1)} %select_reduce_fusion.1.where, bf16[208,16,128]{2,1,0:T(8,128)(2,1)S(1)} %bitcast.13, bf16[256,2048]{1,0:T(8,128)(2,1)S(1)} %copy-done.1, bf16[256,1800]{1,0:T(8,128)(2,1)S(1)} %fusion.pick, f32[8,16,128]{2,1,0:T(8,128)S(1)} %copy-done.4, f32[8,16,128]{2,1,0:T(8,128)S(1)} %copy-done.3), custom_call_target="tpu_custom_call" | custom-call | tf_op jit(solution)/shard_map/score/pallas_call | solution.py:237
  (19 shorter events, 0.1 us)
Async XLA Ops:
  6.5 64.6 %all-gather.2.cloned.1.call-start = ((), (), s32[]{:S(2)}) async-start(), calls=%async_computation.1 | async-start | bytes 1114112 | tf_op jit(solution)/shard_map/all_gather | solution.py:222
  7.7 42.2 %copy-start.13 = (s32[50,36]{0,1:T(8,128)S(1)}, s32[50,36]{0,1:T(8,128)}, u32[]{:S(2)}) copy-start(s32[50,36]{0,1:T(8,128)} %param.22) | copy-start | bytes 21604
  13.0 2.2 %copy-start = (bf16[2,1024,1024]{2,1,0:T(8,128)(2,1)S(1)}, bf16[2,1024,1024]{2,1,0:T(8,128)(2,1)}, u32[]{:S(2)}) copy-start(bf16[2,1024,1024]{2,1,0:T(8,128)(2,1)} %mic.1) | copy-start | bytes 12582916
  15.2 1.0 %copy-start.2 = (bf16[1024,256]{1,0:T(8,128)(2,1)S(1)}, bf16[1024,256]{1,0:T(8,128)(2,1)}, u32[]{:S(2)}) copy-start(bf16[1024,256]{1,0:T(8,128)(2,1)} %constant.87.clone.right_t) | copy-start | bytes 1572868
  16.2 0.8 copy-start.5
  17.1 0.8 copy-start.6
  17.9 0.8 copy-start.7
  18.8 0.8 copy-start.8
  19.6 0.8 copy-start.9
  20.4 0.7 copy-start.10
  21.0 0.7 copy-start.11
  21.7 0.7 copy-start.12
  22.4 48.8 %copy-start.3 = (f32[8,16,128]{2,1,0:T(8,128)S(1)}, f32[8,16,128]{2,1,0:T(8,128)}, u32[]{:S(2)}) copy-start(f32[8,16,128]{2,1,0:T(8,128)} %constant.95.clone.sin_t) | copy-start | bytes 196612
  22.4 48.8 %copy-start.4 = (f32[8,16,128]{2,1,0:T(8,128)S(1)}, f32[8,16,128]{2,1,0:T(8,128)}, u32[]{:S(2)}) copy-start(f32[8,16,128]{2,1,0:T(8,128)} %constant.94.clone.cos_t) | copy-start | bytes 196612
  43.3 27.6 %all-to-all-start = ((bf16[16,13,16,128]{3,2,1,0:T(8,128)(2,1)}), bf16[16,13,16,128]{3,2,1,0:T(8,128)(2,1)S(1)}, u32[]{:S(2)}, u32[]{:S(2)}) async-start(bf16[16,13,16,128]{3,2,1,0:T(8,128)(2,1)} %crop.1), calls=%async_computation | async-start | bytes 1703936 | tf_op jit(solution)/shard_map/all_to_all | solution.py:221
  71.2 1.2 %copy-start.1 = (bf16[256,2048]{1,0:T(8,128)(2,1)S(1)}, bf16[256,2048]{1,0:T(8,128)(2,1)}, u32[]{:S(2)}) copy-start(bf16[256,2048]{1,0:T(8,128)(2,1)} %all-gather.2.cloned.1.call-done.bank) | copy-start | bytes 3145732
Sparse Core Ops, SparseCore 0:
  9.5 38.4 all-gather.1

commit v2 on v1

--- a/solution.py
+++ b/solution.py
@@ -24,9 +24,10 @@
 CHI_SCALE = 0.05
 CHI_SHIFT = 0.1
 
+MESH = pl.DeviceIdType.MESH
 SUB = np.arange(8)[:, None]
 LANE = np.arange(LANES)[None, :]
-TILE_U = (8 * (LANE // K) + SUB - K // 2).astype(np.float64)
+TILE_U = (4 * SUB + LANE // K - K // 2).astype(np.float64)
 TILE_V = (LANE % K + 0 * SUB - K // 2).astype(np.float64)
 
 
@@ -35,7 +36,8 @@
     phase = TWO_PI * np.mod(freq[:, None] * np.arange(BOX)[None, :], BOX) / BOX
     cosine = np.cos(phase) / math.sqrt(BOX)
     sine = -np.sin(phase) / math.sqrt(BOX)
-    left = np.concatenate([cosine, sine], axis=0)
+    order = np.arange(K).reshape(8, K // 8).T.reshape(-1)
+    left = np.concatenate([cosine[order], sine[order]], axis=0)
     right = np.zeros((GROUP, BOX, 2 * GROUP * K))
     for j in range(GROUP):
         right[j, :, j * K : (j + 1) * K] = cosine.T
@@ -62,10 +64,11 @@
     return (n - 1).bit_length()
 
 
-def window_tiles(q, base, slot_cap, label_bits, row_bits, col_bits, info, mic_def, mic, lane_id, row_id, lhs):
+def window_tiles(q, base, shifts, info, mic, lane_id, row_id, lhs):
+    label_bits, row_bits, col_bits = shifts
     scalars = []
-    last_tile = mic.shape[1] // ROWS - 1
-    last_block = mic.shape[2] // LANES - 1
+    last_tile = mic.shape[2] - 1
+    last_block = mic.shape[1] - 1
     for j in range(GROUP):
         packed = lax.shift_right_logical(info[base + j], label_bits)
         left = packed & (2**col_bits - 1)
@@ -78,15 +81,14 @@
         col_f = rl.astype(jnp.float32).astype(jnp.bfloat16)
 
         def column(b):
-            lanes = pl.ds(pl.multiple_of(b * LANES, LANES), LANES)
-            main = mic[m, pl.ds(pl.multiple_of(tile * ROWS, ROWS), BOX), lanes]
-            tail = mic[m, pl.ds(pl.multiple_of(end_tile * ROWS, ROWS), ROWS), lanes]
-            head = jnp.where(row_id[...] >= row_f, main[:ROWS], tail)
+            main = mic[m, b, pl.ds(tile, BOX // ROWS)].reshape(BOX, LANES)
+            tail = mic[m, b, end_tile]
+            head = jnp.where(row_id >= row_f, main[:ROWS], tail)
             return jnp.concatenate([head, main[ROWS:]], axis=0)
 
         first = column(block)
         third = column(jnp.minimum(block + 2, last_block))
-        mask = jnp.broadcast_to(lane_id[...], (BOX, LANES)) >= col_f
+        mask = lane_id >= col_f
         lhs[pl.ds(q * BOX, BOX), pl.ds(2 * j * LANES, LANES)] = jnp.where(mask, first, third)
         lhs[pl.ds(q * BOX, BOX), pl.ds((2 * j + 1) * LANES, LANES)] = column(block + 1)
         scalars.append((m, rt, rl))
@@ -124,26 +126,133 @@
     return tiles
 
 
-def crop_kernel(peers, slot_cap, shifts, info, mic_def, labels, mic, left_t, right_t, prow_c, prow_s,
-                pcol_c, pcol_s, ctf, lane_id, row_id, out, lhs):
+def crop_kernel(peers, slot_cap, shifts, info, mic_def, defocus, shard, mic_h, left_h, right_h, prow_ch, prow_sh,
+                pcol_ch, pcol_sh, arrived, bank, mic, left_t, right_t, prow_c, prow_s, pcol_c, pcol_s, ctf, lhs,
+                padded, outgoing, load_sem, send_sem, recv_sem, local_sem, bank_send, bank_recv):
     groups = slot_cap // GROUP
-
-    def per_peer(peer, carry):
+    depth = peers // 4
+    me = lax.axis_index("dom")
+    my_z, my_y, my_c = me // 4, (me // 2) % 2, me % 2
+
+    loads = [
+        pltpu.make_async_copy(src, dst, load_sem.at[i])
+        for i, (src, dst) in enumerate(
+            [(left_h, left_t), (right_h, right_t), (prow_ch, prow_c), (prow_sh, prow_s),
+             (pcol_ch, pcol_c), (pcol_sh, pcol_s)]
+            + [
+                (mic_h.at[m, :, :, pl.ds(b * LANES, LANES)], mic.at[m, b])
+                for m in range(mic.shape[0])
+                for b in range(mic.shape[1])
+            ]
+        )
+    ]
+    for load in loads:
+        load.start()
+
+    barrier = pltpu.get_barrier_semaphore()
+
+    def greet(k, carry):
+        pl.semaphore_signal(barrier, inc=1, device_id={"dom": (me + k) % peers}, device_id_type=MESH)
+        return carry
+
+    padded[...] = jnp.zeros_like(padded)
+    padded[: shard.shape[0]] = shard[...]
+    lax.fori_loop(1, peers, greet, 0)
+
+    sub = lax.broadcasted_iota(jnp.int32, (8, LANES), 0)
+    lane = lax.broadcasted_iota(jnp.int32, (8, LANES), 1)
+    tile_u = (4 * sub + lane // K - K // 2).astype(jnp.float32)
+    tile_v = (lane % K - K // 2).astype(jnp.float32)
+    radius = tile_u * tile_u + tile_v * tile_v
+    for d in range(defocus.shape[0]):
+        ctf[d] = -jnp.sin(CHI_SCALE * defocus[d] * radius + CHI_SHIFT)
+    lane_id = lax.broadcasted_iota(jnp.int32, (BOX, LANES), 1).astype(jnp.float32).astype(jnp.bfloat16)
+    row_id = lax.broadcasted_iota(jnp.int32, (ROWS, LANES), 0).astype(jnp.float32).astype(jnp.bfloat16)
+    label_lane = lax.broadcasted_iota(jnp.int32, (ROWS, LANES), 1)
+    pl.semaphore_wait(barrier, peers - 1)
+
+    def to_z(d):
+        there = (my_z + d) % depth
+        return pltpu.make_async_remote_copy(
+            src_ref=padded, dst_ref=bank.at[me], send_sem=bank_send.at[d], recv_sem=bank_recv.at[d],
+            device_id={"dom": there * 4 + me % 4}, device_id_type=MESH)
+
+    def to_y(i):
+        row = i * 4 + me % 4
+        return pltpu.make_async_remote_copy(
+            src_ref=bank.at[row], dst_ref=bank.at[row], send_sem=bank_send.at[depth + i],
+            recv_sem=bank_recv.at[depth + i],
+            device_id={"dom": my_z * 4 + (1 - my_y) * 2 + my_c}, device_id_type=MESH)
+
+    def to_c(i):
+        row = i * 2 + my_c
+        return pltpu.make_async_remote_copy(
+            src_ref=bank.at[row], dst_ref=bank.at[row], send_sem=bank_send.at[2 * depth + i],
+            recv_sem=bank_recv.at[2 * depth + i],
+            device_id={"dom": my_z * 4 + my_y * 2 + 1 - my_c}, device_id_type=MESH)
+
+    def each(count, act, first=0):
+        def step(i, carry):
+            act(i)
+            return carry
+
+        lax.fori_loop(first, count, step, 0)
+
+    own = pltpu.make_async_copy(padded, bank.at[me], local_sem.at[0])
+    own.start()
+    each(depth, lambda d: to_z(d).start(), 1)
+    for load in loads:
+        load.wait()
+
+    def peer_of(k):
+        step = k // 4
+        dz = jnp.where(step < depth // 2, depth // 2 + step, depth - 1 - step)
+        return ((my_z + dz) % depth) * 4 + (me + 1 + k) % 4
+
+    def block_copy(k):
+        return pltpu.make_async_remote_copy(
+            src_ref=outgoing.at[k], dst_ref=arrived.at[me], send_sem=send_sem.at[k], recv_sem=recv_sem.at[k],
+            device_id={"dom": peer_of(k)}, device_id_type=MESH)
+
+    def per_peer(k, carry):
+        base = peer_of(k) * slot_cap
         scalars = [
-            window_tiles(q, peer * slot_cap + q * GROUP, slot_cap, *shifts, info, mic_def, mic,
-                         lane_id, row_id, lhs)
-            for q in range(groups)
+            window_tiles(q, base + q * GROUP, shifts, info, mic, lane_id, row_id, lhs) for q in range(groups)
         ]
+
+        @pl.when(k > 0)
+        def _():
+            block_copy(k - 1).start()
+
+        @pl.when(k == peers // 3)
+        def _():
+            own.wait()
+            each(depth, lambda d: to_z(d).wait(), 1)
+            each(depth, lambda i: to_y(i).start())
+
+        @pl.when(k == (2 * peers) // 3)
+        def _():
+            each(depth, lambda i: to_y(i).wait())
+            each(2 * depth, lambda i: to_c(i).start())
+
         first = jnp.dot(lhs[...], right_t[...], preferred_element_type=jnp.float32)
         for q in range(groups):
             tiles = group_windows(first[q * BOX : (q + 1) * BOX], scalars[q], left_t, prow_c, prow_s,
                                   pcol_c, pcol_s, ctf, mic_def)
             for j in range(GROUP):
-                out[peer, q * GROUP + j] = tiles[j]
-        out[peer, slot_cap] = labels[peer]
+                outgoing[k, q * GROUP + j] = tiles[j]
+        labels = jnp.zeros((ROWS, LANES), jnp.int32)
+        for i in range(slot_cap):
+            labels = jnp.where(label_lane == i, info[base + i] & (2 ** shifts[0] - 1), labels)
+        outgoing[k, slot_cap] = labels.astype(jnp.float32).astype(jnp.bfloat16)
         return carry
 
     lax.fori_loop(0, peers, per_peer, 0)
+    mine = pltpu.make_async_copy(outgoing.at[peers - 1], arrived.at[me], local_sem.at[1])
+    mine.start()
+    each(2 * depth, lambda i: to_c(i).wait())
+    each(peers - 1, lambda k: block_copy(k).wait())
+    mine.wait()
 
 
 def score_kernel(where, arrived, bank, pick, cos_t, sin_t, out, lhs):
@@ -167,6 +276,7 @@
 
 
 VMEM = pl.BlockSpec(memory_space=pltpu.VMEM)
+HBM = pl.BlockSpec(memory_space=pl.ANY)
 SMEM = pl.BlockSpec(memory_space=pltpu.SMEM)
 
 
@@ -192,34 +302,37 @@
     packed = (((mic_id << row_bits) + top << col_bits) + left << label_bits) + label
     slots = jnp.arange(peers * slot_cap, dtype=jnp.int32)
     info = jnp.sum(jnp.where(position[None, :] == slots[:, None], packed[None, :], 0), axis=1)
-    labels = (info & (2**label_bits - 1)).astype(jnp.bfloat16).reshape(peers, 1, slot_cap)
-    labels = jnp.broadcast_to(jnp.pad(labels, ((0, 0), (0, 0), (0, LANES - slot_cap))), (peers, ROWS, LANES))
 
     left_t, right_t = dft_tables()
-    radius = jnp.asarray((TILE_U**2 + TILE_V**2).astype(np.float32))
-    ctf = -jnp.sin(CHI_SCALE * defocus[:, None, None] * radius[None] + CHI_SHIFT)
-    lane_id = np.broadcast_to(np.arange(LANES, dtype=np.float32), (ROWS, LANES)).astype(ml_dtypes.bfloat16)
-    row_id = np.broadcast_to(np.arange(ROWS, dtype=np.float32)[:, None], (ROWS, LANES)).astype(ml_dtypes.bfloat16)
-
+    tables = [left_t, right_t] + phase_tables()
     groups = slot_cap // GROUP
-    outgoing = pl.pallas_call(
-        functools.partial(crop_kernel, peers, slot_cap, (label_bits, row_bits, col_bits)),
-        out_shape=jax.ShapeDtypeStruct((peers, slot_cap + 1, ROWS, LANES), jnp.bfloat16),
-        in_specs=[SMEM, SMEM] + [VMEM] * 11,
-        out_specs=VMEM,
-        scratch_shapes=[pltpu.VMEM((groups * BOX, GROUP * BOX), jnp.bfloat16)],
-        compiler_params=pltpu.CompilerParams(vmem_limit_bytes=48 << 20),
-        name="crop",
-    )(info, mic_defocus, labels, micrographs, jnp.asarray(left_t), jnp.asarray(right_t),
-      *[jnp.asarray(t) for t in phase_tables()], ctf, jnp.asarray(lane_id[:1]), jnp.asarray(row_id))
-
     bank_rows, area2 = template_bank.shape
     pad_rows = -(-bank_rows // ROWS) * ROWS
-    shard = template_bank.reshape(bank_rows, 2, K // 8, 8, K).transpose(0, 1, 3, 2, 4).reshape(bank_rows, area2)
-    shard = jnp.pad(shard, ((0, pad_rows - bank_rows), (0, 0)))
-
-    arrived = lax.all_to_all(outgoing, "dom", split_axis=0, concat_axis=0, tiled=True)
-    bank = lax.all_gather(shard, "dom", axis=0, tiled=True)
+    copies = len(tables) + mics * (width // LANES)
+    dma = pltpu.SemaphoreType.DMA
+    arrived, bank = pl.pallas_call(
+        functools.partial(crop_kernel, peers, slot_cap, (label_bits, row_bits, col_bits)),
+        out_shape=(
+            jax.ShapeDtypeStruct((peers, slot_cap + 1, ROWS, LANES), jnp.bfloat16),
+            jax.ShapeDtypeStruct((peers, pad_rows, area2), jnp.bfloat16),
+        ),
+        in_specs=[SMEM, SMEM, SMEM, VMEM] + [HBM] * (1 + len(tables)),
+        out_specs=(HBM, HBM),
+        scratch_shapes=[
+            pltpu.VMEM((mics, width // LANES, height // ROWS, ROWS, LANES), jnp.bfloat16),
+            *[pltpu.VMEM(t.shape, t.dtype) for t in tables],
+            pltpu.VMEM((defocus.shape[0], 8, LANES), jnp.float32),
+            pltpu.VMEM((groups * BOX, GROUP * BOX), jnp.bfloat16),
+            pltpu.VMEM((pad_rows, area2), jnp.bfloat16),
+            pltpu.VMEM((peers, slot_cap + 1, ROWS, LANES), jnp.bfloat16),
+            dma((copies,)), dma((peers,)), dma((peers,)), dma((2,)), dma((peers,)), dma((peers,)),
+        ],
+        compiler_params=pltpu.CompilerParams(
+            collective_id=0, has_side_effects=True, vmem_limit_bytes=56 << 20),
+        name="crop",
+    )(info, mic_defocus, defocus, template_bank,
+      micrographs.reshape(mics, height // ROWS, ROWS, width), *[jnp.asarray(t) for t in tables])
+    bank = bank.reshape(peers * pad_rows, area2)
 
     stride = slot_cap + 1
     got = arrived[:, slot_cap, 0, :slot_cap].astype(jnp.int32)

time: 92 us -> 62.4 us (0.68)
  the two profiles are of different devices: /device:TPU:9 before, /device:TPU:27 now
where the time goes in v2:
time: 62.4 us; the launch traced here: 61.9 us
  Pallas kernels  52.9 us (85%)
  other arithmetic  5.76 us (9%)
  local copies, waits for them, and re-layouts  3.09 us (5%)
    pallas_call x1, Pallas kernels, body(): pl.pallas_call(functools.partial(crop_kernel, peers, slot_cap, (label_bit...  41 us
    pallas_call x1, Pallas kernels, body(): pl.pallas_call(score_kernel, grid=(P_DEV // CHUNK,), out_shape=jax.ShapeD...  12 us
    unnamed x8, local copies, waits for them, and re-layouts  2.38 us

profile of v2, /device:TPU:27, one launch (start us, length us, event | category | flops | bytes accessed | tf_op | source)
XLA Modules:
  0.0 61.9 jit_solution(180990363269759060)
XLA Ops:
  0.0 0.0 copy-start.2
  0.0 0.0 copy-start.3
  0.0 0.8 %fusion.10 = (pred[192]{0:T(512)(128)(4,1)S(1)}, pred[192]{0:T(512)(128)(4,1)S(1)}) fusion(s32[4,192]{1,0:T(4,128)} %param.17), kind=kLoop, calls=%fused_computation.32 | loop fusion | flops 1152 | bytes 1152 | tf_op jit(solution)/shard_map/jit(floor_divide)/and | solution.py:293
  0.8 0.7 %fusion.4 = (s32[1,192]{1,0:T(1,128)S(1)}, s32[1,192]{1,0:T(1,128)S(1)}) fusion(s32[4,192]{1,0:T(4,128)} %param.17), kind=kLoop, calls=%fused_computation.21 | loop fusion | flops 1920 | bytes 2304 | tf_op jit(solution)/shard_map/jit(_where)/select_n | solution.py:293
  1.5 0.2 convert_reduce_fusion
  1.7 0.9 %add_select_fusion.4 = (s32[1,192]{1,0:T(1,128)S(1)}, s32[1,192]{1,0:T(1,128)S(1)}) fusion(s32[1,192]{1,0:T(1,128)S(1)} %bitcast.16, s32[1,192]{1,0:T(1,128)S(1)} %get-tuple-element.11, s32[4,192]{1,0:T(4,128)} %param.17), kind=kLoop, calls=%fused_computation.26 | loop fusion | flops 4032 | bytes 6144 | tf_op jit(solution)/shard_map/jit(_where)/select_n | solution.py:298
  2.5 0.7 %select_reduce_fusion.info = s32[192]{0:T(256)} fusion(s32[192]{0:T(256)S(1)} %bitcast.18, s32[192]{0:T(256)S(1)} %bitcast.17), kind=kLoop, calls=%fused_computation.2 | loop fusion | flops 110400 | bytes 2304 | tf_op jit(solution)/shard_map/reduce_sum | solution.py:304
  3.2 0.7 %sign_compare_fusion = pred[50,36]{0,1:T(8,128)(4,1)S(1)} fusion(s32[50,36]{0,1:T(8,128)} %param.19), kind=kLoop, calls=%fused_computation.8 | loop fusion | flops 3600 | bytes 9000 | tf_op jit(solution)/shard_map/jit(floor_divide)/ne | solution.py:344
  4.0 0.1 copy.19
  4.1 0.1 ne.79
  4.2 0.7 %broadcast_remainder_fusion = (s32[50,36]{0,1:T(8,128)S(1)}, s32[50,36]{0,1:T(8,128)S(1)}) fusion(s32[50,36]{0,1:T(8,128)} %param.19), kind=kLoop, calls=%fused_computation.12 | loop fusion | flops 3600 | bytes 21600 | tf_op jit(solution)/shard_map/jit(floor_divide)/rem | solution.py:344
  5.0 0.1 copy.20
  5.0 0.1 rem.46
  5.2 0.1 copy.21
  5.3 0.1 div.31
  5.4 0.2 fusion.pick
  5.6 41.0 %crop.1 = (bf16[16,13,16,128]{3,2,1,0:T(8,128)(2,1)}, bf16[16,16,2048]{2,1,0:T(8,128)(2,1)}) custom-call(s32[192]{0:T(256)} %select_reduce_fusion.info, s32[2]{0:T(128)} %mic_def.1, f32[16]{0:T(128)} %defocus.1, bf16[14,2048]{1,0:T(8,128)(2,1)} %shard.1, bf16[2,64,16,1024]{3,2,1,0:T(8,128)(2,1)} %bitcast.12, bf16[64,256]{1,0:T(8,128)(2,1)} %constant.71.clone.left_h, ...), custom_call_target="tpu_custom_call" | custom-call | tf_op jit(solution)/shard_map/crop/pallas_call | solution.py:313
  46.5 0.8 %slice_convert_fusion = s32[16,1,1,12]{3,2,1,0:T(1,128)S(1)} fusion(bf16[16,13,16,128]{3,2,1,0:T(8,128)(2,1)} %get-tuple-element.7), kind=kLoop, calls=%fused_computation.16 | loop fusion | flops 192 | bytes 1152 | tf_op jit(solution)/shard_map/convert_element_type | solution.py:338
  47.3 0.1 copy.18
  47.4 0.1 select_reduce_fusion.1.where
  47.5 0.0 copy-done.2
  47.5 0.0 copy-done.3
  47.5 0.0 copy-start
  47.6 1.2 %copy-done = bf16[16,16,2048]{2,1,0:T(8,128)(2,1)S(1)} copy-done((bf16[16,16,2048]{2,1,0:T(8,128)(2,1)S(1)}, bf16[16,16,2048]{2,1,0:T(8,128)(2,1)}, u32[]{:S(2)}) %copy-start) | copy-done | bytes 1048600
  48.8 0.0 copy-start.1
  48.8 1.2 %copy-done.1 = bf16[16,13,16,128]{3,2,1,0:T(8,128)(2,1)S(1)} copy-done((bf16[16,13,16,128]{3,2,1,0:T(8,128)(2,1)S(1)}, bf16[16,13,16,128]{3,2,1,0:T(8,128)(2,1)}, u32[]{:S(2)}) %copy-start.1) | copy-done | bytes 851992
  49.9 12.0 %score.1 = bf16[1536,1800]{1,0:T(8,128)(2,1)} custom-call(s32[96]{0:T(128)S(1)} %select_reduce_fusion.1.where, bf16[208,16,128]{2,1,0:T(8,128)(2,1)S(1)} %bitcast.11, bf16[256,2048]{1,0:T(8,128)(2,1)S(1)} %bitcast.10, bf16[256,1800]{1,0:T(8,128)(2,1)S(1)} %fusion.pick, f32[8,16,128]{2,1,0:T(8,128)S(1)} %copy-done.3, f32[8,16,128]{2,1,0:T(8,128)S(1)} %copy-done.2), custom_call_target="tpu_custom_call" | custom-call | tf_op jit(solution)/shard_map/score/pallas_call | solution.py:350
  (5 shorter events, 0.0 us)
Async XLA Ops:
  0.0 47.5 %copy-start.2 = (f32[8,16,128]{2,1,0:T(8,128)S(1)}, f32[8,16,128]{2,1,0:T(8,128)}, u32[]{:S(2)}) copy-start(f32[8,16,128]{2,1,0:T(8,128)} %constant.78.clone.sin_t) | copy-start | bytes 196612
  0.0 47.5 %copy-start.3 = (f32[8,16,128]{2,1,0:T(8,128)S(1)}, f32[8,16,128]{2,1,0:T(8,128)}, u32[]{:S(2)}) copy-start(f32[8,16,128]{2,1,0:T(8,128)} %constant.77.clone.cos_t) | copy-start | bytes 196612
  47.5 1.2 %copy-start = (bf16[16,16,2048]{2,1,0:T(8,128)(2,1)S(1)}, bf16[16,16,2048]{2,1,0:T(8,128)(2,1)}, u32[]{:S(2)}) copy-start(bf16[16,16,2048]{2,1,0:T(8,128)(2,1)} %get-tuple-element.8) | copy-start | bytes 3145732
  48.8 1.2 %copy-start.1 = (bf16[16,13,16,128]{3,2,1,0:T(8,128)(2,1)S(1)}, bf16[16,13,16,128]{3,2,1,0:T(8,128)(2,1)}, u32[]{:S(2)}) copy-start(bf16[16,13,16,128]{3,2,1,0:T(8,128)(2,1)} %get-tuple-element.7) | copy-start | bytes 2555908

commit v3 on v2

--- a/solution.py
+++ b/solution.py
@@ -19,6 +19,7 @@
 ROWS = 16
 GROUP = 4
 CHUNK = 16
+HALVES = 2
 
 TWO_PI = 2.0 * math.pi
 CHI_SCALE = 0.05
@@ -230,7 +231,7 @@
             each(depth, lambda d: to_z(d).wait(), 1)
             each(depth, lambda i: to_y(i).start())
 
-        @pl.when(k == (2 * peers) // 3)
+        @pl.when(k == peers - 2)
         def _():
             each(depth, lambda i: to_y(i).wait())
             each(2 * depth, lambda i: to_c(i).start())
@@ -255,28 +256,42 @@
     mine.wait()
 
 
-def score_kernel(where, arrived, bank, pick, cos_t, sin_t, out, lhs):
-    base = pl.program_id(0) * CHUNK
-
-    def expand(n, carry):
-        x = arrived[where[base + n]].astype(jnp.float32)
-        rows = pl.ds(pl.multiple_of(n * SHIFTS, SHIFTS), SHIFTS)
-        for k in range(8):
-            re = jnp.broadcast_to(x[k : k + 1], (SHIFTS, LANES))
-            im = jnp.broadcast_to(x[8 + k : 9 + k], (SHIFTS, LANES))
-            c, s = cos_t[k], sin_t[k]
-            lhs[rows, k * LANES : (k + 1) * LANES] = (re * c - im * s).astype(jnp.bfloat16)
-            lhs[rows, (8 + k) * LANES : (9 + k) * LANES] = (re * s + im * c).astype(jnp.bfloat16)
-        return carry
-
-    lax.fori_loop(0, CHUNK, expand, 0, unroll=2)
-    scores = lax.dot_general(lhs[...], bank[...], (((1,), (1,)), ((), ())),
-                             preferred_element_type=jnp.float32).astype(jnp.bfloat16)
-    out[...] = jnp.dot(scores, pick[...], preferred_element_type=jnp.float32).astype(jnp.bfloat16)
+def score_kernel(where, arrived, bank, pick, cos_t, sin_t, out, *halves):
+    base = pl.program_id(0) * CHUNK * len(halves)
+
+    def expand(half, lhs):
+        for n in range(CHUNK):
+            x = arrived[where[base + half * CHUNK + n]].astype(jnp.float32)
+            rows = slice(n * SHIFTS, (n + 1) * SHIFTS)
+            for k in range(8):
+                re = jnp.broadcast_to(x[k : k + 1], (SHIFTS, LANES))
+                im = jnp.broadcast_to(x[8 + k : 9 + k], (SHIFTS, LANES))
+                c, s = cos_t[k], sin_t[k]
+                lhs[rows, k * LANES : (k + 1) * LANES] = (re * c - im * s).astype(jnp.bfloat16)
+                lhs[rows, (8 + k) * LANES : (9 + k) * LANES] = (re * s + im * c).astype(jnp.bfloat16)
+
+    def score(lhs):
+        return lax.dot_general(lhs[...], bank[...], (((1,), (1,)), ((), ())),
+                               preferred_element_type=jnp.float32).astype(jnp.bfloat16)
+
+    def emit(half, scores):
+        rows = CHUNK * SHIFTS
+        picked = jnp.dot(scores, pick[...], preferred_element_type=jnp.float32)
+        out[half * rows : (half + 1) * rows] = picked.astype(jnp.bfloat16)
+
+    waiting = None
+    for half, lhs in enumerate(halves):
+        expand(half, lhs)
+        scores = score(lhs)
+        if waiting is not None:
+            emit(half - 1, waiting)
+        waiting = scores
+    emit(len(halves) - 1, waiting)
 
 
 VMEM = pl.BlockSpec(memory_space=pltpu.VMEM)
-HBM = pl.BlockSpec(memory_space=pl.ANY)
+HBM = pl.BlockSpec(memory_space=pltpu.HBM)
+ANY = pl.BlockSpec(memory_space=pl.ANY)
 SMEM = pl.BlockSpec(memory_space=pltpu.SMEM)
 
 
@@ -317,7 +332,7 @@
             jax.ShapeDtypeStruct((peers, pad_rows, area2), jnp.bfloat16),
         ),
         in_specs=[SMEM, SMEM, SMEM, VMEM] + [HBM] * (1 + len(tables)),
-        out_specs=(HBM, HBM),
+        out_specs=(ANY, ANY),
         scratch_shapes=[
             pltpu.VMEM((mics, width // LANES, height // ROWS, ROWS, LANES), jnp.bfloat16),
             *[pltpu.VMEM(t.shape, t.dtype) for t in tables],
@@ -341,7 +356,7 @@
     where = jnp.sum(jnp.where(got[None] == wanted[:, None, None], at[None], 0), axis=(1, 2))
 
     flat = rot_index.reshape(-1)
-    entry = flat // bank_rows * pad_rows + flat % bank_rows
+    entry = flat + lax.div(flat, jnp.int32(bank_rows)) * (pad_rows - bank_rows)
     templates = flat.shape[0]
     pick = (jnp.arange(peers * pad_rows, dtype=jnp.int32)[:, None] == entry[None, :]).astype(jnp.bfloat16)
 
@@ -349,7 +364,7 @@
     full = lambda shape: pl.BlockSpec(shape, lambda i: (0,) * len(shape), pipeline_mode=pl.Buffered(1))
     out = pl.pallas_call(
         score_kernel,
-        grid=(P_DEV // CHUNK,),
+        grid=(P_DEV // (HALVES * CHUNK),),
         out_shape=jax.ShapeDtypeStruct((P_DEV * SHIFTS, templates), jnp.bfloat16),
         in_specs=[
             SMEM,
@@ -359,9 +374,9 @@
             full((8, SHIFTS, LANES)),
             full((8, SHIFTS, LANES)),
         ],
-        out_specs=pl.BlockSpec((CHUNK * SHIFTS, templates), lambda i: (i, 0)),
-        scratch_shapes=[pltpu.VMEM((CHUNK * SHIFTS, area2), jnp.bfloat16)],
-        compiler_params=pltpu.CompilerParams(vmem_limit_bytes=48 << 20),
+        out_specs=pl.BlockSpec((HALVES * CHUNK * SHIFTS, templates), lambda i: (i, 0)),
+        scratch_shapes=[pltpu.VMEM((CHUNK * SHIFTS, area2), jnp.bfloat16)] * HALVES,
+        compiler_params=pltpu.CompilerParams(vmem_limit_bytes=56 << 20),
         name="score",
     )(where, arrived.reshape(peers * stride, ROWS, LANES), bank, pick, jnp.asarray(cos_t), jnp.asarray(sin_t))
     return out.reshape(P_DEV, SHIFTS, templates)

time: 62.4 us -> 53.7 us (0.86)
  Pallas kernels: 52.9 us -> 46.5 us
  local copies, waits for them, and re-layouts: 3.09 us -> 1 us
    pallas_call x1, Pallas kernels: 12 us -> 8.65 us  [body(): pl.pallas_call(score_kernel, grid=(P_DEV // (HALVES * CHUNK),), out_shape...]
    pallas_call x1, Pallas kernels: 41 us -> 37.8 us  [body(): pl.pallas_call(functools.partial(crop_kernel, peers, slot_cap, (label_bit...]
    unnamed x8 -> x1, local copies, waits for them, and re-layouts: 2.38 us -> 0.82 us
    convert_element_type x1, other arithmetic: 0.18 us -> 1.18 us  [body(): (jnp.arange(peers * pad_rows, dtype=jnp.int32)[:, None] == entry[None, :]...]
    rem x1 -> x0, other arithmetic: 0.74 us -> none  [body(): entry = flat // bank_rows * pad_rows + flat % bank_rows]
    ne x1 -> x0, other arithmetic: 0.74 us -> none  [body(): entry = flat // bank_rows * pad_rows + flat % bank_rows]
where the time goes in v3:
time: 53.7 us; the launch traced here: 53.3 us
  Pallas kernels  46.5 us (87%)
  other arithmetic  5.82 us (11%)
  local copies, waits for them, and re-layouts  1 us (2%)
    pallas_call x1, Pallas kernels, body(): pl.pallas_call(functools.partial(crop_kernel, peers, slot_cap, (label_bit...  37.8 us
    pallas_call x1, Pallas kernels, body(): pl.pallas_call(score_kernel, grid=(P_DEV // (HALVES * CHUNK),), out_shape...  8.65 us
    convert_element_type x1, other arithmetic, body(): (jnp.arange(peers * pad_rows, dtype=jnp.int32)[:, None] == entry[None, :]...  1.18 us

profile of v3, /device:TPU:27, one launch (start us, length us, event | category | flops | bytes accessed | tf_op | source)
XLA Modules:
  0.0 53.3 jit_solution(9256201624652956909)
XLA Ops:
  0.0 0.7 %fusion.8 = (pred[192]{0:T(512)(128)(4,1)S(1)}, pred[192]{0:T(512)(128)(4,1)S(1)}) fusion(s32[4,192]{1,0:T(4,128)} %param.17), kind=kLoop, calls=%fused_computation.26 | loop fusion | flops 1152 | bytes 1152 | tf_op jit(solution)/shard_map/jit(floor_divide)/and | solution.py:308
  0.7 0.7 %fusion.2 = (s32[1,192]{1,0:T(1,128)S(1)}, s32[1,192]{1,0:T(1,128)S(1)}) fusion(s32[4,192]{1,0:T(4,128)} %param.17), kind=kLoop, calls=%fused_computation.15 | loop fusion | flops 1920 | bytes 2304 | tf_op jit(solution)/shard_map/jit(_where)/select_n | solution.py:308
  1.4 0.2 convert_reduce_fusion
  1.6 0.9 %add_select_fusion.2 = (s32[1,192]{1,0:T(1,128)S(1)}, s32[1,192]{1,0:T(1,128)S(1)}) fusion(s32[1,192]{1,0:T(1,128)S(1)} %bitcast.16, s32[1,192]{1,0:T(1,128)S(1)} %get-tuple-element.11, s32[4,192]{1,0:T(4,128)} %param.17), kind=kLoop, calls=%fused_computation.20 | loop fusion | flops 4032 | bytes 6144 | tf_op jit(solution)/shard_map/jit(_where)/select_n | solution.py:313
  2.5 0.7 %select_reduce_fusion.info = s32[192]{0:T(256)} fusion(s32[192]{0:T(256)S(1)} %bitcast.18, s32[192]{0:T(256)S(1)} %bitcast.17), kind=kLoop, calls=%fused_computation.2 | loop fusion | flops 110400 | bytes 2304 | tf_op jit(solution)/shard_map/reduce_sum | solution.py:319
  3.2 0.8 %copy.17 = s32[50,36]{1,0:T(8,128)S(1)} copy(s32[50,36]{0,1:T(8,128)} %param.19) | data formatting | bytes 14400 | tf_op args[5]
  4.0 0.1 reshape.99
  4.1 1.2 %fusion.pick = bf16[256,1800]{1,0:T(8,128)(2,1)} fusion(s32[1800]{0:T(1024)S(1)} %multiply_add_fusion), kind=kLoop, calls=%fused_computation.1 | loop fusion | flops 921600 | bytes 928800 | tf_op jit(solution)/shard_map/convert_element_type | solution.py:361
  5.3 37.8 %crop.1 = (bf16[16,13,16,128]{3,2,1,0:T(8,128)(2,1)}, bf16[16,16,2048]{2,1,0:T(8,128)(2,1)}) custom-call(s32[192]{0:T(256)} %select_reduce_fusion.info, s32[2]{0:T(128)} %mic_def.1, f32[16]{0:T(128)} %defocus.1, bf16[14,2048]{1,0:T(8,128)(2,1)} %shard.1, bf16[2,64,16,1024]{3,2,1,0:T(8,128)(2,1)} %bitcast.10, bf16[64,256]{1,0:T(8,128)(2,1)} %constant.56.clone.left_h, ...), custom_call_target="tpu_custom_call" | custom-call | tf_op jit(solution)/shard_map/crop/pallas_call | solution.py:328
  43.1 0.8 %slice_convert_fusion = s32[16,1,1,12]{3,2,1,0:T(1,128)S(1)} fusion(bf16[16,13,16,128]{3,2,1,0:T(8,128)(2,1)} %get-tuple-element.7), kind=kLoop, calls=%fused_computation.10 | loop fusion | flops 192 | bytes 1152 | tf_op jit(solution)/shard_map/convert_element_type | solution.py:353
  43.9 0.1 copy.16
  44.0 0.7 %select_reduce_fusion.1.where = s32[96]{0:T(128)} fusion(s32[16,12]{0,1:T(8,128)S(1)} %iota_add_fusion, s32[96]{0:T(128)S(1)} %iota_add_fusion.1, s32[16,12]{0,1:T(8,128)S(1)} %copy.16), kind=kLoop, calls=%fused_computation.7 | loop fusion | flops 55200 | bytes 2304 | tf_op jit(solution)/shard_map/reduce_sum | solution.py:356
  44.7 8.7 %score.1 = bf16[1536,1800]{1,0:T(8,128)(2,1)} custom-call(s32[96]{0:T(128)} %select_reduce_fusion.1.where, bf16[208,16,128]{2,1,0:T(8,128)(2,1)} %bitcast.12, bf16[256,2048]{1,0:T(8,128)(2,1)} %bitcast.11, bf16[256,1800]{1,0:T(8,128)(2,1)} %fusion.pick, f32[8,16,128]{2,1,0:T(8,128)} %constant.62.clone.cos_t, f32[8,16,128]{2,1,0:T(8,128)} %constant.63.clone.sin_t), custom_call_target="tpu_custom_call" | custom-call | tf_op jit(solution)/shard_map/score/pallas_call | solution.py:365
  (5 shorter events, 0.0 us)
